TPU v7x, 256 devices: a whole 4x4x8 slice. The times are simulated.
256 devices in a mesh: ctx: 8 (over y, x_hi), chan: 32 (over x_lo, z, core).
Axes of the slice: x: 4 (x_hi: 2, x_lo: 2; x = x_hi * 2 + x_lo), y: 4, z: 8, core: 2. Of those that a mesh axis runs over, the one named last changes fastest.
Arguments:
- token_ids: int32 [2048], P('ctx'), may hold values from 0 to 511
- embed_table: bfloat16 [512, 8192], P(None, 'chan'), may hold values from -6 to 6
- in_weight: bfloat16 [8192, 3, 8192], P(None, None, 'chan'), may hold values from -0.0625 to 0.0625
- feat_taps: float32 [3, 3, 8192], P(None, None, 'chan'), may hold values from -3.5 to 3.5
- modal_rates: float32 [16, 512], P(None, 'chan'), may hold values from 4.8828126e-05 to 0.03
- modal_residues: float32 [16, 512], P(None, 'chan'), may hold values from -1.5 to 1.5
- out_grad: bfloat16 [2048, 8192], P('ctx', 'chan'), may hold values from -6 to 6
Outputs:
- output: bfloat16 [2048, 8192], P('ctx', 'chan')
- grad_tokens: bfloat16 [2048, 8192], P('ctx', 'chan')
All inputs are finite; a program needn't handle non-finite values.
Results may differ from a plain program's by a relative error of at most 0.034.
Values may be sent and summed in bfloat16 or wider, within the bound.
No kernel may reach another device: no remote copies, remote signals or barrier semaphores. Data moves between devices by JAX's collectives and lax.ppermute only.
A program may use at most 128 MiB of HBM per device.

v0:
```python
import jax
import jax.numpy as jnp
from jax import lax
from jax.sharding import PartitionSpec as P

GROUP = 16
ORDER = 16
FEAT = 3
exact_mode = lax.Precision.HIGHEST


def passed_along(value, axis, by):
    count = lax.axis_size(axis)
    pairs = [(i, i + by) for i in range(count) if 0 <= i + by < count]
    return lax.ppermute(value, axis, pairs)


def neighbour_rows(pieces, offset):
    return passed_along(pieces, "ctx", offset)


def featurize_local(stream, taps):
    length = stream.shape[0]
    tail_rows = neighbour_rows(stream[length - (FEAT - 1) :], 1)
    widened = jnp.concatenate([tail_rows, stream], axis=0).astype(jnp.float32)
    summed = jnp.zeros(stream.shape, jnp.float32)
    for tap_index in range(FEAT):
        begin = FEAT - 1 - tap_index
        summed = summed + taps[:, tap_index, :][None] * widened[begin : begin + length]
    return summed


def featurize_back(stream, taps):
    length = stream.shape[0]
    head_rows = neighbour_rows(stream[: FEAT - 1], -1)
    widened = jnp.concatenate([stream, head_rows], axis=0).astype(jnp.float32)
    summed = jnp.zeros(stream.shape, jnp.float32)
    for tap_index in range(FEAT):
        summed = summed + taps[:, tap_index, :][None] * widened[tap_index : tap_index + length]
    return summed


def modal_tables(block_rates, block_gains, length):
    positions = jnp.arange(length, dtype=jnp.float32)
    powers = jnp.exp(-positions[:, None, None] * block_rates[None])
    growth = jnp.exp(positions[:, None, None] * block_rates[None])
    weighted = powers * block_gains[None]
    full_table = jnp.einsum("tog,sog->tsg", weighted, growth, precision=exact_mode)
    causal = (
        jnp.arange(length, dtype=jnp.int32)[:, None] >= jnp.arange(length, dtype=jnp.int32)[None, :]
    )
    toeplitz = jnp.where(causal[:, :, None], full_table, 0.0)
    start_weights = weighted * jnp.exp(-block_rates)[None]
    end_powers = jnp.exp(-(float(length - 1) - positions)[:, None, None] * block_rates[None])
    return (toeplitz, start_weights, end_powers)


def modal_block(sequence, tables):
    toeplitz, start_weights, end_powers = tables
    local_part = jnp.einsum("tsg,sgc->tgc", toeplitz, sequence, precision=exact_mode)
    end_state = jnp.einsum("sog,sgc->ogc", end_powers, sequence, precision=exact_mode)
    return (local_part, end_state)


def modal_apply(sequence, modal_rates, modal_residues, backward):
    length, channels = sequence.shape
    groups = channels // GROUP
    gain_terms = modal_residues * jnp.sqrt(-jnp.expm1(-2.0 * modal_rates))
    shaped = sequence.reshape(length, groups, GROUP)
    ctx_devices = lax.axis_size("ctx")
    share_groups = groups // ctx_devices
    exchanged = lax.all_to_all(
        shaped.astype(jnp.bfloat16), "ctx", split_axis=1, concat_axis=0, tiled=True
    ).astype(shaped.dtype)
    first_group = lax.axis_index("ctx") * share_groups
    own_rates = lax.dynamic_slice_in_dim(modal_rates, first_group, share_groups, 1)
    own_gains = lax.dynamic_slice_in_dim(gain_terms, first_group, share_groups, 1)
    if backward:
        exchanged = jnp.flip(exchanged, 0)
    pieces = exchanged.reshape(ctx_devices, length, share_groups, GROUP)
    tables = modal_tables(own_rates, own_gains, length)
    block_decay = jnp.exp(-own_rates * length)[:, :, None]

    def advance(carried, piece):
        local_part, end_state = modal_block(piece, tables)
        result = local_part + jnp.einsum("tog,ogc->tgc", tables[1], carried, precision=exact_mode)
        return (block_decay * carried + end_state, result)

    start_state = jnp.zeros((ORDER, share_groups, GROUP), jnp.float32)
    _, block_outs = lax.scan(advance, start_state, pieces)
    whole_out = block_outs.reshape(ctx_devices * length, share_groups, GROUP)
    if backward:
        whole_out = jnp.flip(whole_out, 0)
    returned = lax.all_to_all(
        whole_out.astype(jnp.bfloat16), "ctx", split_axis=0, concat_axis=1, tiled=True
    ).astype(whole_out.dtype)
    return returned.reshape(length, channels)


def body(token_ids, embed_table, in_weight, feat_taps, modal_rates, modal_residues, out_grad):
    length = token_ids.shape[0]
    vocab_size = embed_table.shape[0]
    model_width = in_weight.shape[0]
    channels = in_weight.shape[2]
    flat_weight = in_weight.reshape(model_width, 3 * channels)
    one_hot = (token_ids[:, None] == jnp.arange(vocab_size, dtype=jnp.int32)[None, :]).astype(
        jnp.bfloat16
    )
    own_features = jnp.dot(one_hot, embed_table, preferred_element_type=jnp.float32).astype(
        jnp.bfloat16
    )
    rows_used = flat_weight
    projected = jnp.dot(
        lax.all_gather(own_features, "chan", axis=1, tiled=True),
        rows_used,
        preferred_element_type=jnp.float32,
    )
    stream = projected.reshape(length, 3, channels).astype(jnp.bfloat16)
    stream = lax.optimization_barrier(stream)
    featured = featurize_local(stream, feat_taps)
    query_rows = featured[:, 0]
    key_rows = featured[:, 1]
    value_rows = featured[:, 2]
    mixed_rows = key_rows * value_rows
    long_conv = modal_apply(mixed_rows, modal_rates, modal_residues, False)
    output = (query_rows * long_conv).astype(jnp.bfloat16)
    grad_rows = out_grad.astype(jnp.float32)
    grad_query = grad_rows * long_conv
    grad_long = grad_rows * query_rows
    grad_mixed = modal_apply(grad_long, modal_rates, modal_residues, True)
    grad_feat = jnp.stack(
        [grad_query, grad_mixed * value_rows, grad_mixed * key_rows], axis=1
    ).astype(jnp.bfloat16)
    grad_feat = lax.optimization_barrier(grad_feat)
    grad_proj = (
        featurize_back(grad_feat, feat_taps).astype(jnp.bfloat16).reshape(length, 3 * channels)
    )
    rows_used = flat_weight
    summed_rows = lax.psum_scatter(
        lax.dot_general(
            rows_used, grad_proj, (((1,), (1,)), ((), ())), preferred_element_type=jnp.float32
        ).astype(jnp.bfloat16),
        "chan",
        scatter_dimension=0,
        tiled=True,
    ).astype(jnp.float32)
    return (output, summed_rows.T.astype(jnp.bfloat16))


def solution(mesh):
    in_specs = (
        P("ctx"),
        P(None, "chan"),
        P(None, None, "chan"),
        P(None, None, "chan"),
        P(None, "chan"),
        P(None, "chan"),
        P("ctx", "chan"),
    )
    out_specs = (P("ctx", "chan"), P("ctx", "chan"))
    return jax.shard_map(body, mesh=mesh, in_specs=in_specs, out_specs=out_specs, check_vma=False)
```

profile of v0, /device:TPU:8, one launch (start us, length us, event | category | flops | bytes accessed | tf_op | source)
XLA Modules:
  0.0 326.2 jit_solution(7893675662903279602)
XLA Ops:
  7.2 0.9 copy-done
  8.1 1.6 convolution_convert_fusion
  9.8 0.8 constant_dynamic-slice_fusion.1
  10.7 16.7 %copy.55 = bf16[8192,3,256]{0,2,1:T(8,128)(2,1)} copy(bf16[8192,3,256]{2,0,1:T(8,128)(2,1)} %param.13) | data formatting | bytes 25165824 | tf_op args[2]
  27.5 58.0 %all-gather.2.cloned.1.call-done = bf16[256,8192]{1,0:T(8,128)(2,1)} async-done(((bf16[256,256]{1,0:T(8,128)(2,1)}), bf16[256,8192]{1,0:T(8,128)(2,1)}) %all-gather.2.cloned.1.call-update) | async-done | bytes 4194320 | tf_op jit(solution)/shard_map/all_gather | solution.py:114
  85.5 9.3 %fusion.58 = bf16[256,3,256]{2,0,1:T(8,128)(2,1)S(1)} fusion(bf16[8192,3,256]{0,2,1:T(8,128)(2,1)} %copy.55, bf16[256,8192]{1,0:T(8,128)(2,1)} %all-gather.2.cloned.1.call-done), kind=kOutput, calls=%fused_computation.61 | convolution fusion | flops 3221422080 | bytes 17170432 | tf_op jit(solution)/shard_map/dot_general | solution.py:113
  94.8 4.9 %collective-permute-start = (bf16[2,3,256]{2,0,1:T(2,128)(2,1)S(1)}, bf16[2,3,256]{2,0,1:T(2,128)(2,1)S(1)}, u32[]{:S(2)}, u32[]{:S(2)}) collective-permute-start(bf16[2,3,256]{2,0,1:T(2,128)(2,1)S(1)} %slice.59), channel_id=1, source_target_pairs={{0,32},{32,64},{64,96},{96,128},{128,160},{160,192},{192,224},{1,3... | collective-permute-start | bytes 9224 | tf_op jit(solution)/shard_map/ppermute | solution.py:15
  99.7 3.0 collective-permute-done
  103.9 6.3 %all-to-all-start.2 = ((bf16[256,16,16]{0,2,1:T(8,128)(2,1)}), bf16[256,16,16]{0,2,1:T(8,128)(2,1)S(1)}, u32[]{:S(2)}, u32[]{:S(2)}) async-start(bf16[256,16,16]{0,2,1:T(8,128)(2,1)} %bitcast.14), calls=%async_computation.2 | async-start | bytes 262144 | tf_op jit(solution)/shard_map/all_to_all | solution.py:72
  111.1 5.6 %all-to-all-done.2 = bf16[256,16,16]{0,2,1:T(8,128)(2,1)S(1)} async-done(((bf16[256,16,16]{0,2,1:T(8,128)(2,1)}), bf16[256,16,16]{0,2,1:T(8,128)(2,1)S(1)}, u32[]{:S(2)}, u32[]{:S(2)}) %all-to-all-start.2) | async-done | bytes 131104 | tf_op jit(solution)/shard_map/all_to_all | solution.py:72
  116.9 1.2 rev.7
  118.2 10.2 %while.31 = (s32[]{:T(128)}, f32[16,2,16]{0,2,1:T(8,128)S(1)}, bf16[8,256,2,16]{1,0,3,2:T(8,128)(2,1)S(1)}, f32[16,2,1]{0,1,2:T(2,128)S(1)}, f32[8,256,2,16]{1,0...) while((s32[]{:T(128)}, f32[16,2,16]{0,2,1:T(8,128)S(1)}, ...), condition=%wide.region_3.4_spmd.clone.clone.clone, body=%wide.region_2.3_spmd.clone.clone.clone.sunk | while | flops 28362756 | bytes 811800 | solution.py:90
  128.4 1.3 rev.8
  130.5 1.1 reshape.99
  131.6 10.6 %all_to_all.16 = bf16[8,2,4096]{2,1,0:T(2,128)(2,1)S(1)} all-to-all(bf16[8,2,4096]{2,1,0:T(2,128)(2,1)S(1)} %reshape.99), channel_id=1, replica_groups=mesh['ctx'=8,'chan'=32] {'ctx'}, dimensions={0} | all-to-all | bytes 262144 | tf_op jit(solution)/shard_map/all_to_all | solution.py:94
  144.8 4.9 %all-to-all-start = ((bf16[256,16,16]{0,2,1:T(8,128)(2,1)}), bf16[256,16,16]{0,2,1:T(8,128)(2,1)S(1)}, u32[]{:S(2)}, u32[]{:S(2)}) async-start(bf16[256,16,16]{0,2,1:T(8,128)(2,1)} %bitcast.6), calls=%async_computation | async-start | bytes 262144 | tf_op jit(solution)/shard_map/all_to_all | solution.py:72
  149.7 6.6 %all-to-all-done = bf16[256,16,16]{0,2,1:T(8,128)(2,1)S(1)} async-done(((bf16[256,16,16]{0,2,1:T(8,128)(2,1)}), bf16[256,16,16]{0,2,1:T(8,128)(2,1)S(1)}, u32[]{:S(2)}, u32[]{:S(2)}) %all-to-all-start) | async-done | bytes 131104 | tf_op jit(solution)/shard_map/all_to_all | solution.py:72
  156.3 8.4 %while.30 = (s32[]{:T(128)}, f32[16,2,16]{0,2,1:T(8,128)S(1)}, bf16[8,256,2,16]{1,3,2,0:T(8,128)(2,1)S(1)}, f32[16,2,1]{0,1,2:T(2,128)S(1)}, f32[8,256,2,16]{1,3...) while((s32[]{:T(128)}, f32[16,2,16]{0,2,1:T(8,128)S(1)}, ...), condition=%wide.region_1.2_spmd.clone.clone.clone, body=%wide.region_0.1_spmd.clone.clone.clone.sunk | while | flops 28354564 | bytes 730268 | solution.py:90
  165.4 1.1 reshape.97
  166.5 10.6 %all_to_all.17 = bf16[8,2,4096]{2,1,0:T(2,128)(2,1)S(1)} all-to-all(bf16[8,2,4096]{2,1,0:T(2,128)(2,1)S(1)} %reshape.97), channel_id=1, replica_groups=mesh['ctx'=8,'chan'=32] {'ctx'}, dimensions={0} | all-to-all | bytes 262144 | tf_op jit(solution)/shard_map/all_to_all | solution.py:94
  179.5 3.7 %collective-permute-start.1 = (bf16[2,3,256]{2,0,1:T(2,128)(2,1)S(1)}, bf16[2,3,256]{2,0,1:T(2,128)(2,1)S(1)}, u32[]{:S(2)}, u32[]{:S(2)}) collective-permute-start(bf16[2,3,256]{2,0,1:T(2,128)(2,1)S(1)} %slice.66), channel_id=1, source_target_pairs={{32,0},{64,32},{96,64},{128,96},{160,128},{192,160},{224,192},{33,... | collective-permute-start | bytes 9224 | tf_op jit(solution)/shard_map/ppermute | solution.py:15
  183.3 3.3 %collective-permute-done.1 = bf16[2,3,256]{2,0,1:T(2,128)(2,1)S(1)} collective-permute-done((bf16[2,3,256]{2,0,1:T(2,128)(2,1)S(1)}, bf16[2,3,256]{2,0,1:T(2,128)(2,1)S(1)}, u32[]{:S(2)}, u32[]{:S(2)}) %collective-permute-start.1) | collective-permute-done | bytes 3104 | tf_op jit(solution)/shard_map/ppermute | solution.py:15
  186.6 14.1 %fusion.56 = bf16[8192,256]{0,1:T(8,128)(2,1)} fusion(bf16[8192,3,256]{2,0,1:T(8,128)(2,1)} %param.13, f32[258,3,256]{2,0,1:T(8,128)S(1)} %maximum_convert_fusion.1, f32[3,256]{1,0:T(4,128)S(1)} %get-tuple-element.441, f32[3,256]{1,0:T(4,128)S(1)} %get-tuple-element.442, f32[3,256]{1,0:T(4,128)S(1)} %bitcast.160), kind=kOutput, calls=%fused_computation.59 | convolution fusion | flops 3224502272 | bytes 19148800 | tf_op jit(solution)/shard_map/dot_general | solution.py:140
  200.7 118.7 %reduce-scatter.2.cloned.1.call-done = bf16[256,256]{0,1:T(8,128)(2,1)} async-done(((bf16[8192,256]{0,1:T(8,128)(2,1)}), bf16[256,256]{0,1:T(8,128)(2,1)}) %reduce-scatter.2.cloned.1.call-update) | async-done | bytes 131088 | tf_op jit(solution)/shard_map/reduce_scatter | solution.py:139
  (125 shorter events, 27.0 us)
Async XLA Ops:
  7.2 1.0 copy-start
  7.2 78.3 %all-gather.2.cloned.1.call-start = ((), (), s32[]{:S(2)}) async-start(), calls=%async_computation.5 | async-start | bytes 4325376 | tf_op jit(solution)/shard_map/all_gather | solution.py:114
  10.7 16.8 %copy-start.2 = (f32[3,3,256]{2,1,0:T(4,128)S(1)}, f32[3,3,256]{2,1,0:T(4,128)}, u32[]{:S(2)}) copy-start(f32[3,3,256]{2,1,0:T(4,128)} %param.14) | copy-start | bytes 27652
  27.5 75.6 %copy-start.1 = (bf16[256,256]{1,0:T(8,128)(2,1)S(1)}, bf16[256,256]{1,0:T(8,128)(2,1)}, u32[]{:S(2)}) copy-start(bf16[256,256]{1,0:T(8,128)(2,1)} %param.17) | copy-start | bytes 393220
  94.8 7.9 %collective-permute-start = (bf16[2,3,256]{2,0,1:T(2,128)(2,1)S(1)}, bf16[2,3,256]{2,0,1:T(2,128)(2,1)S(1)}, u32[]{:S(2)}, u32[]{:S(2)}) collective-permute-start(bf16[2,3,256]{2,0,1:T(2,128)(2,1)S(1)} %slice.59), channel_id=1, source_target_pairs={{0,32},{32,64},{64,96},{96,128},{128,160},{160,192},{192,224},{1,3... | collective-permute-start | bytes 9224 | tf_op jit(solution)/shard_map/ppermute | solution.py:15
  103.9 12.9 %all-to-all-start.2 = ((bf16[256,16,16]{0,2,1:T(8,128)(2,1)}), bf16[256,16,16]{0,2,1:T(8,128)(2,1)S(1)}, u32[]{:S(2)}, u32[]{:S(2)}) async-start(bf16[256,16,16]{0,2,1:T(8,128)(2,1)} %bitcast.14), calls=%async_computation.2 | async-start | bytes 262144 | tf_op jit(solution)/shard_map/all_to_all | solution.py:72
  144.8 11.5 %all-to-all-start = ((bf16[256,16,16]{0,2,1:T(8,128)(2,1)}), bf16[256,16,16]{0,2,1:T(8,128)(2,1)S(1)}, u32[]{:S(2)}, u32[]{:S(2)}) async-start(bf16[256,16,16]{0,2,1:T(8,128)(2,1)} %bitcast.6), calls=%async_computation | async-start | bytes 262144 | tf_op jit(solution)/shard_map/all_to_all | solution.py:72
  149.7 169.7 %reduce-scatter.2.cloned.1.call-start = ((), (), s32[]{:S(2)}) async-start(), calls=%async_computation.6 | async-start | bytes 4325376 | tf_op jit(solution)/shard_map/reduce_scatter | solution.py:139
  179.5 7.0 %collective-permute-start.1 = (bf16[2,3,256]{2,0,1:T(2,128)(2,1)S(1)}, bf16[2,3,256]{2,0,1:T(2,128)(2,1)S(1)}, u32[]{:S(2)}, u32[]{:S(2)}) collective-permute-start(bf16[2,3,256]{2,0,1:T(2,128)(2,1)S(1)} %slice.66), channel_id=1, source_target_pairs={{32,0},{64,32},{96,64},{128,96},{160,128},{192,160},{224,192},{33,... | collective-permute-start | bytes 9224 | tf_op jit(solution)/shard_map/ppermute | solution.py:15
Sparse Core Ops, SparseCore 0:
  10.4 75.1 all-gather.1
  200.8 118.5 reduce-scatter.1
where the time goes:
time: 327 us; the launch traced here: 326 us
  waiting for transfers between devices  195 us (60%)
  matrix products  41.9 us (13%)
  local copies, waits for them, and re-layouts  31.7 us (10%)
  blocking collectives  21.2 us (6%)
  starting transfers between devices  19.9 us (6%)
  between operations  14.4 us (4%)
    reduce_scatter x1, waiting for transfers between devices, body(): lax.psum_scatter(lax.dot_general(rows_used, grad_proj, (((1,), (1,)), (()...  119 us
    all_gather x1, waiting for transfers between devices, body(): lax.all_gather(own_features, 'chan', axis=1, tiled=True)  58 us
    unnamed x19, local copies, waits for them, and re-layouts  21.8 us
    all_to_all x2, blocking collectives, modal_apply(): lax.all_to_all(whole_out.astype(jnp.bfloat16), 'ctx', split_axis=0, conca...  21.2 us
    dot_general x1, matrix products, body(): lax.dot_general(rows_used, grad_proj, (((1,), (1,)), ((), ())), preferred...  14.1 us
    all_to_all x2, waiting for transfers between devices, modal_apply(): lax.all_to_all(shaped.astype(jnp.bfloat16), 'ctx', split_axis=1, concat_a...  12.2 us
    all_to_all x2, starting transfers between devices, modal_apply(): lax.all_to_all(shaped.astype(jnp.bfloat16), 'ctx', split_axis=1, concat_a...  11.2 us
    dot_general x1, matrix products, body(): jnp.dot(lax.all_gather(own_features, 'chan', axis=1, tiled=True), rows_us...  9.3 us
  transfers between devices with their start and end apart: 6, of which 6 were waited for; matrix products, arithmetic and copies ran while one was open for 6% of the time, Pallas kernels for 0%

commit v1 on v0

--- a/solution.py
+++ b/solution.py
@@ -111,7 +111,15 @@
     )
     rows_used = flat_weight
     projected = jnp.dot(
-        lax.all_gather(own_features, "chan", axis=1, tiled=True),
+        jnp.concatenate(
+            lax.all_to_all(
+                jnp.stack([own_features for _ in range(lax.axis_size("chan"))], 0),
+                "chan",
+                split_axis=0,
+                concat_axis=0,
+            ),
+            axis=1,
+        ),
         rows_used,
         preferred_element_type=jnp.float32,
     )

time: 327 us -> 373 us (1.14)
  waiting for transfers between devices: 195 us -> 217 us
  local copies, waits for them, and re-layouts: 31.7 us -> 47.2 us
  starting transfers between devices: 19.9 us -> 29.4 us
    all_to_all x0 -> x1, waiting for transfers between devices: none -> 78.3 us  [body(): lax.all_to_all(jnp.stack([own_features for _ in range(lax.axis_size('chan...]
    all_gather x1 -> x0, waiting for transfers between devices: 58 us -> none  [body(): lax.all_gather(own_features, 'chan', axis=1, tiled=True)]
    reshape x0 -> x2, local copies, waits for them, and re-layouts: none -> 13.9 us  [body(): jnp.concatenate(lax.all_to_all(jnp.stack([own_features for _ in range(lax...]
    all_to_all x0 -> x1, starting transfers between devices: none -> 9.91 us  [body(): lax.all_to_all(jnp.stack([own_features for _ in range(lax.axis_size('chan...]
    unnamed x19 -> x23, local copies, waits for them, and re-layouts: 21.8 us -> 21.7 us
  transfers between devices with their start and end apart: 6 -> 6, of which waited for: 6 -> 6; matrix products, arithmetic and copies ran while one was open for 6% -> 5% of each run, Pallas kernels for 0% -> 0%
where the time goes in v1:
time: 373 us; the launch traced here: 372 us
  waiting for transfers between devices  217 us (58%)
  local copies, waits for them, and re-layouts  47.2 us (13%)
  matrix products  41.2 us (11%)
  starting transfers between devices  29.4 us (8%)
  blocking collectives  21.2 us (6%)
  between operations  14.4 us (4%)
    reduce_scatter x1, waiting for transfers between devices, body(): lax.psum_scatter(lax.dot_general(rows_used, grad_proj, (((1,), (1,)), (()...  120 us
    all_to_all x1, waiting for transfers between devices, body(): lax.all_to_all(jnp.stack([own_features for _ in range(lax.axis_size('chan...  78.3 us
    unnamed x23, local copies, waits for them, and re-layouts  21.7 us
    all_to_all x2, blocking collectives, modal_apply(): lax.all_to_all(whole_out.astype(jnp.bfloat16), 'ctx', split_axis=0, conca...  21.2 us
    dot_general x1, matrix products, body(): lax.dot_general(rows_used, grad_proj, (((1,), (1,)), ((), ())), preferred...  14.1 us
    reshape x2, local copies, waits for them, and re-layouts, body(): jnp.concatenate(lax.all_to_all(jnp.stack([own_features for _ in range(lax...  13.9 us
    all_to_all x2, waiting for transfers between devices, modal_apply(): lax.all_to_all(shaped.astype(jnp.bfloat16), 'ctx', split_axis=1, concat_a...  12.2 us
    all_to_all x2, starting transfers between devices, modal_apply(): lax.all_to_all(shaped.astype(jnp.bfloat16), 'ctx', split_axis=1, concat_a...  11.1 us
  transfers between devices with their start and end apart: 6, of which 6 were waited for; matrix products, arithmetic and copies ran while one was open for 5% of the time, Pallas kernels for 0%

profile of v1, /device:TPU:8, one launch (start us, length us, event | category | flops | bytes accessed | tf_op | source)
XLA Modules:
  0.0 372.2 jit_solution(8570081349677935740)
XLA Ops:
  9.1 2.4 stack.8
  11.5 9.9 %all-to-all-start = ((bf16[32,256,256]{2,1,0:T(8,128)(2,1)}), bf16[32,256,256]{2,1,0:T(8,128)(2,1)}, u32[]{:S(2)}, u32[]{:S(2)}) async-start(bf16[32,256,256]{2,1,0:T(8,128)(2,1)} %stack.8), calls=%async_computation | async-start | bytes 8388608 | tf_op jit(solution)/shard_map/all_to_all | solution.py:115
  21.7 16.6 %copy.57 = bf16[8192,3,256]{0,2,1:T(8,128)(2,1)} copy(bf16[8192,3,256]{2,0,1:T(8,128)(2,1)} %param.13) | data formatting | bytes 25165824 | tf_op args[2]
  38.4 78.3 %all-to-all-done = bf16[32,256,256]{2,1,0:T(8,128)(2,1)} async-done(((bf16[32,256,256]{2,1,0:T(8,128)(2,1)}), bf16[32,256,256]{2,1,0:T(8,128)(2,1)}, u32[]{:S(2)}, u32[]{:S(2)}) %all-to-all-start) | async-done | bytes 4194336 | tf_op jit(solution)/shard_map/all_to_all | solution.py:115
  116.7 6.5 %copy.56 = bf16[256,32,256]{2,1,0:T(8,128)(2,1)} copy(bf16[256,32,256]{2,0,1:T(8,128)(2,1)} %bitcast) | data formatting | bytes 8388608 | tf_op jit(solution)/shard_map/reshape | solution.py:114
  123.2 7.4 %reshape.105 = bf16[256,8192,1]{1,0,2:T(8,128)(2,1)} reshape(bf16[256,32,256]{2,1,0:T(8,128)(2,1)} %copy.56) | data formatting | bytes 8388608 | tf_op jit(solution)/shard_map/reshape | solution.py:114
  130.6 9.3 %fusion.57 = bf16[256,3,256]{2,0,1:T(8,128)(2,1)S(1)} fusion(bf16[256,8192,1]{1,0,2:T(8,128)(2,1)} %reshape.105, bf16[8192,3,256]{0,2,1:T(8,128)(2,1)} %copy.57), kind=kOutput, calls=%fused_computation.60 | convolution fusion | flops 3221422080 | bytes 17170432 | tf_op jit(solution)/shard_map/dot_general | solution.py:113
  140.0 4.6 %collective-permute-start = (bf16[2,3,256]{2,0,1:T(2,128)(2,1)S(1)}, bf16[2,3,256]{2,0,1:T(2,128)(2,1)S(1)}, u32[]{:S(2)}, u32[]{:S(2)}) collective-permute-start(bf16[2,3,256]{2,0,1:T(2,128)(2,1)S(1)} %slice.59), channel_id=1, source_target_pairs={{0,32},{32,64},{64,96},{96,128},{128,160},{160,192},{192,224},{1,3... | collective-permute-start | bytes 9224 | tf_op jit(solution)/shard_map/ppermute | solution.py:15
  144.6 3.2 collective-permute-done
  149.0 6.2 %all-to-all-start.3 = ((bf16[256,16,16]{0,2,1:T(8,128)(2,1)}), bf16[256,16,16]{0,2,1:T(8,128)(2,1)S(1)}, u32[]{:S(2)}, u32[]{:S(2)}) async-start(bf16[256,16,16]{0,2,1:T(8,128)(2,1)} %bitcast.14), calls=%async_computation.3 | async-start | bytes 262144 | tf_op jit(solution)/shard_map/all_to_all | solution.py:72
  156.1 5.6 %all-to-all-done.3 = bf16[256,16,16]{0,2,1:T(8,128)(2,1)S(1)} async-done(((bf16[256,16,16]{0,2,1:T(8,128)(2,1)}), bf16[256,16,16]{0,2,1:T(8,128)(2,1)S(1)}, u32[]{:S(2)}, u32[]{:S(2)}) %all-to-all-start.3) | async-done | bytes 131104 | tf_op jit(solution)/shard_map/all_to_all | solution.py:72
  161.9 1.2 rev.7
  163.2 10.2 %while.31 = (s32[]{:T(128)}, f32[16,2,16]{0,2,1:T(8,128)S(1)}, bf16[8,256,2,16]{1,0,3,2:T(8,128)(2,1)S(1)}, f32[16,2,1]{0,1,2:T(2,128)S(1)}, f32[8,256,2,16]{1,0...) while((s32[]{:T(128)}, f32[16,2,16]{0,2,1:T(8,128)S(1)}, ...), condition=%wide.region_3.4_spmd.clone.clone.clone, body=%wide.region_2.3_spmd.clone.clone.clone.sunk | while | flops 28362756 | bytes 811800 | solution.py:90
  173.4 1.3 rev.8
  175.5 1.1 reshape.110
  176.5 10.6 %all_to_all.20 = bf16[8,2,4096]{2,1,0:T(2,128)(2,1)S(1)} all-to-all(bf16[8,2,4096]{2,1,0:T(2,128)(2,1)S(1)} %reshape.110), channel_id=1, replica_groups=mesh['ctx'=8,'chan'=32] {'ctx'}, dimensions={0} | all-to-all | bytes 262144 | tf_op jit(solution)/shard_map/all_to_all | solution.py:94
  189.7 4.9 %all-to-all-start.1 = ((bf16[256,16,16]{0,2,1:T(8,128)(2,1)}), bf16[256,16,16]{0,2,1:T(8,128)(2,1)S(1)}, u32[]{:S(2)}, u32[]{:S(2)}) async-start(bf16[256,16,16]{0,2,1:T(8,128)(2,1)} %bitcast.6), calls=%async_computation.1 | async-start | bytes 262144 | tf_op jit(solution)/shard_map/all_to_all | solution.py:72
  194.6 6.6 %all-to-all-done.1 = bf16[256,16,16]{0,2,1:T(8,128)(2,1)S(1)} async-done(((bf16[256,16,16]{0,2,1:T(8,128)(2,1)}), bf16[256,16,16]{0,2,1:T(8,128)(2,1)S(1)}, u32[]{:S(2)}, u32[]{:S(2)}) %all-to-all-start.1) | async-done | bytes 131104 | tf_op jit(solution)/shard_map/all_to_all | solution.py:72
  201.2 8.4 %while.30 = (s32[]{:T(128)}, f32[16,2,16]{0,2,1:T(8,128)S(1)}, bf16[8,256,2,16]{1,3,2,0:T(8,128)(2,1)S(1)}, f32[16,2,1]{0,1,2:T(2,128)S(1)}, f32[8,256,2,16]{1,3...) while((s32[]{:T(128)}, f32[16,2,16]{0,2,1:T(8,128)S(1)}, ...), condition=%wide.region_1.2_spmd.clone.clone.clone, body=%wide.region_0.1_spmd.clone.clone.clone.sunk | while | flops 28354564 | bytes 730268 | solution.py:90
  211.4 10.6 %all_to_all.42 = bf16[8,2,4096]{2,1,0:T(2,128)(2,1)S(1)} all-to-all(bf16[8,2,4096]{2,1,0:T(2,128)(2,1)S(1)} %reshape.108), channel_id=1, replica_groups=mesh['ctx'=8,'chan'=32] {'ctx'}, dimensions={0} | all-to-all | bytes 262144 | tf_op jit(solution)/shard_map/all_to_all | solution.py:94
  224.5 3.7 collective-permute-start.1
  228.2 3.3 collective-permute-done.1
  231.5 14.1 %fusion.56 = bf16[8192,256]{0,1:T(8,128)(2,1)} fusion(bf16[8192,3,256]{2,0,1:T(8,128)(2,1)} %param.13, f32[258,3,256]{2,0,1:T(8,128)S(1)} %maximum_convert_fusion.1, f32[3,256]{1,0:T(4,128)S(1)} %get-tuple-element.441, f32[3,256]{1,0:T(4,128)S(1)} %get-tuple-element.442, f32[3,256]{1,0:T(4,128)S(1)} %bitcast.157), kind=kOutput, calls=%fused_computation.59 | convolution fusion | flops 3224502272 | bytes 19148800 | tf_op jit(solution)/shard_map/dot_general | solution.py:148
  245.6 119.8 %reduce-scatter.2.cloned.1.call-done = bf16[256,256]{0,1:T(8,128)(2,1)} async-done(((bf16[8192,256]{0,1:T(8,128)(2,1)}), bf16[256,256]{0,1:T(8,128)(2,1)}) %reduce-scatter.2.cloned.1.call-update) | async-done | bytes 131088 | tf_op jit(solution)/shard_map/reduce_scatter | solution.py:147
  (131 shorter events, 29.9 us)
Async XLA Ops:
  7.2 1.0 copy-start
  7.2 14.2 %copy-start.2 = (f32[16,16]{1,0:T(8,128)S(1)}, f32[16,16]{1,0:T(8,128)}, u32[]{:S(2)}) copy-start(f32[16,16]{1,0:T(8,128)} %param.16) | copy-start | bytes 3076
  7.2 14.2 %copy-start.3 = (f32[16,16]{1,0:T(8,128)S(1)}, f32[16,16]{1,0:T(8,128)}, u32[]{:S(2)}) copy-start(f32[16,16]{1,0:T(8,128)} %param.15) | copy-start | bytes 3076
  11.5 105.2 %all-to-all-start = ((bf16[32,256,256]{2,1,0:T(8,128)(2,1)}), bf16[32,256,256]{2,1,0:T(8,128)(2,1)}, u32[]{:S(2)}, u32[]{:S(2)}) async-start(bf16[32,256,256]{2,1,0:T(8,128)(2,1)} %stack.8), calls=%async_computation | async-start | bytes 8388608 | tf_op jit(solution)/shard_map/all_to_all | solution.py:115
  21.7 16.7 %copy-start.4 = (f32[3,3,256]{2,1,0:T(4,128)S(1)}, f32[3,3,256]{2,1,0:T(4,128)}, u32[]{:S(2)}) copy-start(f32[3,3,256]{2,1,0:T(4,128)} %param.14) | copy-start | bytes 27652
  130.6 17.6 %copy-start.1 = (bf16[256,256]{1,0:T(8,128)(2,1)S(1)}, bf16[256,256]{1,0:T(8,128)(2,1)}, u32[]{:S(2)}) copy-start(bf16[256,256]{1,0:T(8,128)(2,1)} %param.17) | copy-start | bytes 393220
  140.0 7.9 %collective-permute-start = (bf16[2,3,256]{2,0,1:T(2,128)(2,1)S(1)}, bf16[2,3,256]{2,0,1:T(2,128)(2,1)S(1)}, u32[]{:S(2)}, u32[]{:S(2)}) collective-permute-start(bf16[2,3,256]{2,0,1:T(2,128)(2,1)S(1)} %slice.59), channel_id=1, source_target_pairs={{0,32},{32,64},{64,96},{96,128},{128,160},{160,192},{192,224},{1,3... | collective-permute-start | bytes 9224 | tf_op jit(solution)/shard_map/ppermute | solution.py:15
  149.0 12.7 %all-to-all-start.3 = ((bf16[256,16,16]{0,2,1:T(8,128)(2,1)}), bf16[256,16,16]{0,2,1:T(8,128)(2,1)S(1)}, u32[]{:S(2)}, u32[]{:S(2)}) async-start(bf16[256,16,16]{0,2,1:T(8,128)(2,1)} %bitcast.14), calls=%async_computation.3 | async-start | bytes 262144 | tf_op jit(solution)/shard_map/all_to_all | solution.py:72
  189.7 11.5 %all-to-all-start.1 = ((bf16[256,16,16]{0,2,1:T(8,128)(2,1)}), bf16[256,16,16]{0,2,1:T(8,128)(2,1)S(1)}, u32[]{:S(2)}, u32[]{:S(2)}) async-start(bf16[256,16,16]{0,2,1:T(8,128)(2,1)} %bitcast.6), calls=%async_computation.1 | async-start | bytes 262144 | tf_op jit(solution)/shard_map/all_to_all | solution.py:72
  194.6 170.8 %reduce-scatter.2.cloned.1.call-start = ((), (), s32[]{:S(2)}) async-start(), calls=%async_computation.6 | async-start | bytes 4325376 | tf_op jit(solution)/shard_map/reduce_scatter | solution.py:147
  224.5 7.0 %collective-permute-start.1 = (bf16[2,3,256]{2,0,1:T(2,128)(2,1)S(1)}, bf16[2,3,256]{2,0,1:T(2,128)(2,1)S(1)}, u32[]{:S(2)}, u32[]{:S(2)}) collective-permute-start(bf16[2,3,256]{2,0,1:T(2,128)(2,1)S(1)} %slice.66), channel_id=1, source_target_pairs={{32,0},{64,32},{96,64},{128,96},{160,128},{192,160},{224,192},{33,... | collective-permute-start | bytes 9224 | tf_op jit(solution)/shard_map/ppermute | solution.py:15
Sparse Core Ops, SparseCore 0:
  245.7 119.6 reduce-scatter.1
